TPU v7x, 32 devices: a whole 2x2x4 slice. The times are simulated.
32 devices in a mesh: groups: 2 (over x), freq: 16 (over z, y, core).
Axes of the slice: x: 2, y: 2, z: 4, core: 2. Of those that a mesh axis runs over, the one named last changes fastest.
Arguments:
- dyson: bfloat16 [128, 4, 2, 512, 512], P(('groups', 'freq')), parts along dimension 0, may hold values from -2.1 to 2.1
- guess: bfloat16 [128, 4, 2, 512, 512], P(('groups', 'freq')), parts along dimension 0, may hold values from -2 to 2
- coulomb: bfloat16 [1024, 512], P('groups'), parts along dimension 0, may hold values from -3 to 3
- partner: int32 [4], replicated, may hold values from 0 to 3, as said below
- freq_index: int32 [2, 64], replicated, may hold values from -128 to 127
Outputs:
- screened: bfloat16 [128, 4, 2, 512, 512], P(('groups', 'freq')), parts along dimension 0
There are 2 independent parts, one for each index of `groups`. A program takes and returns all parts, laid end to end along the dimension named above; an argument that names none is the same for every part. Nothing has to cross between parts.
Inputs may be any that keep to these rules, and one draw needn't show every extreme that they name: partner is a permutation of the 4 lattice vectors.
All inputs are finite; a program needn't handle non-finite values.
Results may differ from a plain program's by a relative error of at most 0.0069.
Values may be sent and summed in bfloat16 or wider, within the bound.
A program may use at most 256 MiB of HBM per device.

v0:
```python
import math

import jax
import jax.numpy as jnp
from jax import lax
from jax.sharding import PartitionSpec as P

NT = 64


def fermion_table(freq_index, time_count):
    freq_count = freq_index.shape[1]
    odd_freq = 2 * freq_index[0] + 1
    odd_time = 2 * jnp.arange(time_count, dtype=jnp.int32) + 1
    phases = jnp.mod(odd_time[:, None] * odd_freq[None, :], 4 * time_count)
    angles = phases.astype(jnp.float32) * (math.pi / (2 * time_count))
    cosine = jnp.cos(angles) / math.sqrt(freq_count)
    sine_part = jnp.sin(angles) / math.sqrt(freq_count)
    real_rows = jnp.stack([cosine, sine_part], axis=-1)
    imag_rows = jnp.stack([-sine_part, cosine], axis=-1)
    return jnp.stack([real_rows, imag_rows], axis=1).astype(jnp.bfloat16)


def boson_table(freq_index, time_count):
    odd_time = 2 * jnp.arange(time_count, dtype=jnp.int32) + 1
    phases = jnp.mod(freq_index[1][:, None] * odd_time[None, :], 2 * time_count)
    angles = phases.astype(jnp.float32) * (math.pi / time_count)
    cosine = jnp.cos(angles) / math.sqrt(time_count)
    sine_part = jnp.sin(angles) / math.sqrt(time_count)
    real_rows = jnp.stack([cosine, -sine_part], axis=-1)
    imag_rows = jnp.stack([sine_part, cosine], axis=-1)
    return jnp.stack([real_rows, imag_rows], axis=1).astype(jnp.bfloat16)


def batched(left_matrix, right_matrix):
    return jnp.einsum("bij,bjk->bik", left_matrix, right_matrix, preferred_element_type=jnp.float32)


def newton_green(dyson, guess):
    full_shape = dyson.shape
    batch_size = full_shape[0] * full_shape[1]
    matrix_size = full_shape[3]
    flat_dyson = dyson.reshape(batch_size, 2, matrix_size, matrix_size)
    flat_guess = guess.reshape(batch_size, 2, matrix_size, matrix_size)
    dyson_real, dyson_imag = (flat_dyson[:, 0], flat_dyson[:, 1])
    guess_real, guess_imag = (flat_guess[:, 0], flat_guess[:, 1])
    product_real = batched(dyson_real, guess_real) - batched(dyson_imag, guess_imag)
    product_imag = batched(dyson_real, guess_imag) + batched(dyson_imag, guess_real)
    unit_matrix = jnp.eye(matrix_size, dtype=jnp.float32)
    corr_real = (2.0 * unit_matrix - product_real).astype(jnp.bfloat16)
    corr_imag = (-product_imag).astype(jnp.bfloat16)
    green_real = batched(guess_real, corr_real) - batched(guess_imag, corr_imag)
    green_imag = batched(guess_real, corr_imag) + batched(guess_imag, corr_real)
    green_freq = jnp.stack([green_real, green_imag], axis=1).astype(jnp.bfloat16)
    return green_freq.reshape(full_shape)


def to_time(phase_table, values):
    return jnp.einsum("tdwc,wrcse->trdse", phase_table, values, preferred_element_type=jnp.float32)


def to_freq(phase_table, values):
    return jnp.einsum("vdtc,trcse->vrdse", phase_table, values, preferred_element_type=jnp.float32)


def polarize(green_time, hole_time):
    green_real, green_imag = (green_time[:, :, 0], green_time[:, :, 1])
    hole_real, hole_imag = (hole_time[:, :, 0], hole_time[:, :, 1])
    polar_real = green_real * hole_real - green_imag * hole_imag
    polar_imag = green_real * hole_imag + green_imag * hole_real
    return jnp.stack([polar_real, polar_imag], axis=2).astype(jnp.bfloat16)


def screen_block(polar_freq, coulomb):
    screened_polar = jnp.einsum(
        "ij,frcjk->frcik", coulomb, polar_freq, preferred_element_type=jnp.float32
    )
    screened_polar = screened_polar.astype(jnp.bfloat16)
    product = jnp.einsum(
        "frcij,jk->frcik", screened_polar, coulomb, preferred_element_type=jnp.float32
    )
    real_mask = (jnp.arange(2) == 0).astype(jnp.float32)[None, None, :, None, None]
    return (product + real_mask * coulomb.astype(jnp.float32)[None, None, None]).astype(
        jnp.bfloat16
    )


def local(dyson, guess, coulomb, partner, freq_index):
    green_freq = newton_green(dyson, guess)
    forward = fermion_table(freq_index, NT)
    backward = boson_table(freq_index, NT)
    hole_freq = jnp.swapaxes(jnp.take(green_freq, partner, axis=1), 3, 4)
    green_part = lax.all_to_all(green_freq, "freq", split_axis=3, concat_axis=0, tiled=True)
    hole_part = lax.all_to_all(hole_freq, "freq", split_axis=3, concat_axis=0, tiled=True)
    green_time = to_time(forward, green_part)
    hole_time = to_time(forward, hole_part)[::-1]
    polar_freq = to_freq(backward, polarize(green_time, hole_time)).astype(jnp.bfloat16)
    return screen_block(
        lax.all_to_all(polar_freq, "freq", split_axis=0, concat_axis=3, tiled=True), coulomb
    )


def solution(mesh):
    in_specs = (
        P(("groups", "freq"), None, None, None, None),
        P(("groups", "freq"), None, None, None, None),
        P("groups", None),
        P(),
        P(),
    )
    out_specs = P(("groups", "freq"), None, None, None, None)
    return jax.shard_map(local, mesh=mesh, in_specs=in_specs, out_specs=out_specs, check_vma=False)
```

profile of v0, /device:TPU:13, one launch (start us, length us, event | category | flops | bytes accessed | tf_op | source)
XLA Modules:
  0.0 1658.2 jit_solution(4939689650576631327)
XLA Ops:
  0.2 16.7 %copy.48 = bf16[4,4,2,512,512]{4,3,1,0,2:T(8,128)(2,1)} copy(bf16[4,4,2,512,512]{4,3,2,1,0:T(8,128)(2,1)} %param.6) | data formatting | bytes 33554432 | tf_op args[1]
  16.8 6.5 copy.47
  23.4 16.0 fusion.25
  39.4 16.0 fusion.22
  55.5 15.5 subtract_convert_fusion.2
  70.9 12.8 fusion.27
  83.7 15.9 negate_convert_fusion
  99.6 13.3 fusion.26
  112.8 18.1 %subtract_convert_fusion.1 = bf16[16,512,512]{2,1,0:T(8,128)(2,1)} fusion(f32[16,512,512]{2,1,0:T(8,128)} %fusion.27, bf16[16,512,512]{2,1,0:T(8,128)(2,1)} %negate_convert_fusion, bf16[16,2,512,512]{3,2,0,1:T(8,128)(2,1)} %bitcast.150), kind=kOutput, calls=%fused_computation.27 | convolution fusion | flops 4303355904 | bytes 41943040 | tf_op jit(solution)/shard_map/bij,bjk->bik/dot_general | solution.py:36
  131.0 40.2 %copy.53 = bf16[4,4,1,512,512]{4,2,1,0,3:T(2,128)(2,1)} copy(bf16[4,4,1,512,512]{3,4,1,0,2:T(8,128)(2,1)} %bitcast.162) | data formatting | bytes 16777216 | tf_op jit(solution)/shard_map/stack | solution.py:54
  171.1 18.2 %add_convert_fusion.2 = bf16[16,512,512]{2,1,0:T(8,128)(2,1)} fusion(f32[16,512,512]{2,1,0:T(8,128)} %fusion.26, bf16[16,512,512]{2,1,0:T(8,128)(2,1)} %subtract_convert_fusion.2, bf16[16,2,512,512]{3,2,0,1:T(8,128)(2,1)} %bitcast.151), kind=kOutput, calls=%fused_computation.26 | convolution fusion | flops 4303355904 | bytes 41943040 | tf_op jit(solution)/shard_map/bij,bjk->bik/dot_general | solution.py:36
  189.3 39.3 %copy.54 = bf16[4,4,1,512,512]{4,2,1,0,3:T(2,128)(2,1)} copy(bf16[4,4,1,512,512]{3,4,1,0,2:T(8,128)(2,1)} %bitcast.161) | data formatting | bytes 16777216 | tf_op jit(solution)/shard_map/stack | solution.py:54
  228.6 40.9 %pad_maximum_fusion = bf16[4,4,2,512,512]{4,2,1,0,3:T(2,128)(2,1)} fusion(bf16[4,4,1,512,512]{4,2,1,0,3:T(2,128)(2,1)} %copy.54, bf16[4,4,1,512,512]{4,2,1,0,3:T(2,128)(2,1)} %copy.53), kind=kLoop, calls=%fused_computation.49 | loop fusion | flops 33554432 | bytes 33554432 | tf_op jit(solution)/shard_map/stack | solution.py:54
  269.5 6.9 all-to-all-start
  276.4 47.7 %slice_maximum_fusion.1 = (bf16[4,4,2,256,512]{4,2,1,0,3:T(2,128)(2,1)}, bf16[4,4,2,256,512]{4,2,1,0,3:T(2,128)(2,1)}) fusion(bf16[4,4,1,512,512]{4,2,1,0,3:T(2,128)(2,1)} %copy.54, bf16[4,4,1,512,512]{4,2,1,0,3:T(2,128)(2,1)} %copy.53), kind=kLoop, calls=%fused_computation.35 | loop fusion | flops 33554432 | bytes 33554432 | tf_op jit(solution)/shard_map/stack | solution.py:54
  324.1 8.5 broadcast.498.clone2.1
  332.6 56.2 %while.2 = (s32[]{:T(128)}, bf16[4,4,2,256,512]{4,2,1,0,3:T(2,128)(2,1)}, s32[4,1]{0,1:T(1,128)S(1)}, bf16[4,4,2,256,512]{3,2,0,1,4:T(2,128)(2,1)}, s32[]{:T(128)}) while((s32[]{:T(128)}, bf16[4,4,2,256,512]{4,2,1,0,3:T(2,128)(2,1)}, s32[4,1]{0,1:T(1,128)S(1)}, bf16[4,4,2,256,512]{3,2,0,1,4:T(2,128)(2,1)}, s32[]{:T(128)}) %tuple.47), condition=%wide.while_cond, body=%wide.while_body.sunk | while | flops 2 | bytes 16777804 | solution.py:92
  333.2 3.7 constant_dynamic-slice_fusion.9
  338.9 4.9 copy.99
  343.8 2.8 constant_dynamic-update-slice_fusion.4
  347.2 3.7 constant_dynamic-slice_fusion.9
  352.9 4.9 copy.99
  357.8 2.9 constant_dynamic-update-slice_fusion.4
  361.3 3.7 constant_dynamic-slice_fusion.9
  367.0 4.9 copy.99
  371.9 2.9 constant_dynamic-update-slice_fusion.4
  375.4 3.7 constant_dynamic-slice_fusion.9
  381.0 4.9 copy.99
  386.0 2.9 constant_dynamic-update-slice_fusion.4
  388.8 8.5 broadcast.498.clone2
  397.3 56.0 %while.3 = (s32[]{:T(128)}, bf16[4,4,2,256,512]{4,2,1,0,3:T(2,128)(2,1)}, s32[4,1]{0,1:T(1,128)S(1)}, bf16[4,4,2,256,512]{3,2,0,1,4:T(2,128)(2,1)}, s32[]{:T(128)}) while((s32[]{:T(128)}, bf16[4,4,2,256,512]{4,2,1,0,3:T(2,128)(2,1)}, s32[4,1]{0,1:T(1,128)S(1)}, bf16[4,4,2,256,512]{3,2,0,1,4:T(2,128)(2,1)}, s32[]{:T(128)}) %tuple.50), condition=%wide.while_cond.1, body=%wide.while_body.1.sunk | while | flops 2 | bytes 16777804 | solution.py:92
  397.9 3.7 constant_dynamic-slice_fusion.11
  403.6 4.9 copy.101
  411.9 3.7 constant_dynamic-slice_fusion.11
  417.6 4.9 copy.101
  422.5 2.8 constant_dynamic-update-slice_fusion.5
  425.9 3.7 constant_dynamic-slice_fusion.11
  431.6 4.9 copy.101
  436.5 2.8 constant_dynamic-update-slice_fusion.5
  439.9 3.7 constant_dynamic-slice_fusion.11
  445.6 4.9 copy.101
  450.5 2.8 constant_dynamic-update-slice_fusion.5
  453.3 22.3 %fusion.11 = bf16[4,4,2,512,512]{4,2,1,0,3:T(2,128)(2,1)} fusion(bf16[4,4,2,256,512]{3,2,1,0,4:T(2,128)(2,1)} %bitcast.163, bf16[4,4,2,256,512]{3,2,1,0,4:T(2,128)(2,1)} %bitcast.164, pred[4]{0:T(512)(128)(4,1)S(1)} %compare_and_fusion), kind=kLoop, calls=%fused_computation.30 | loop fusion | flops 41943040 | bytes 33554436 | tf_op jit(solution)/shard_map/jit(_take)/select_n | solution.py:92
  475.6 162.7 %all-to-all-done = bf16[4,4,2,512,512]{4,2,1,0,3:T(2,128)(2,1)} async-done(((bf16[4,4,2,512,512]{4,2,1,0,3:T(2,128)(2,1)}), bf16[4,4,2,512,512]{4,2,1,0,3:T(2,128)(2,1)}, u32[]{:S(2)}, u32[]{:S(2)}) %all-to-all-start) | async-done | bytes 16777248 | tf_op jit(solution)/shard_map/all_to_all | solution.py:93
  638.4 5.3 all-to-all-start.1
  644.2 13.6 copy.93
  657.8 23.6 %reshape.485 = bf16[64,4,2,32,512,1]{4,0,2,3,1,5:T(8,128)(2,1)} reshape(bf16[16,4,4,2,32,512]{5,1,0,3,4,2:T(4,128)(2,1)} %bitcast.158) | data formatting | bytes 33554432 | tf_op jit(solution)/shard_map/all_to_all | solution.py:93
  681.4 324.0 %all-to-all-done.1 = bf16[4,4,2,512,512]{4,2,1,0,3:T(2,128)(2,1)} async-done(((bf16[4,4,2,512,512]{4,2,1,0,3:T(2,128)(2,1)}), bf16[4,4,2,512,512]{4,2,1,0,3:T(2,128)(2,1)}, u32[]{:S(2)}, u32[]{:S(2)}) %all-to-all-start.1) | async-done | bytes 16777248 | tf_op jit(solution)/shard_map/all_to_all | solution.py:94
  1005.4 11.0 copy.60
  1016.4 36.0 %copy.61 = bf16[16,4,4,2,32,512]{5,1,0,3,4,2:T(4,128)(2,1)} copy(bf16[16,4,4,2,32,512]{5,4,0,3,2,1:T(8,128)(2,1)S(1)} %bitcast.159) | data formatting | bytes 33554432 | tf_op jit(solution)/shard_map/all_to_all | solution.py:94
  1052.4 23.7 %reshape.488 = bf16[64,4,2,32,512,1]{4,0,2,3,1,5:T(8,128)(2,1)} reshape(bf16[16,4,4,2,32,512]{5,1,0,3,4,2:T(4,128)(2,1)} %copy.61) | data formatting | bytes 33554432 | tf_op jit(solution)/shard_map/all_to_all | solution.py:94
  1076.1 19.5 %fusion.12 = f32[64,4,2,32,512]{4,0,2,3,1:T(8,128)} fusion(bf16[64,4,2,32,512,1]{4,0,2,3,1,5:T(8,128)(2,1)} %reshape.485, bf16[64,1,64,2]{2,0,3,1:T(8,128)(2,1)S(1)} %get-tuple-element.62, bf16[64,1,64,2]{2,0,3,1:T(8,128)(2,1)S(1)} %get-tuple-element.61), kind=kOutput, calls=%fused_computation.31 | convolution fusion | flops 2147549184 | bytes 50364416 | tf_op jit(solution)/shard_map/tdwc,wrcse->trdse/dot_general | solution.py:59
  1095.6 19.4 %fusion.15 = f32[64,4,2,32,512]{4,0,2,3,1:T(8,128)} fusion(bf16[64,4,2,32,512,1]{4,0,2,3,1,5:T(8,128)(2,1)} %reshape.488, bf16[64,1,64,2]{2,0,3,1:T(8,128)(2,1)S(1)} %get-tuple-element.62, bf16[64,1,64,2]{2,0,3,1:T(8,128)(2,1)S(1)} %get-tuple-element.61), kind=kOutput, calls=%fused_computation.32 | convolution fusion | flops 2147549184 | bytes 50364416 | tf_op jit(solution)/shard_map/tdwc,wrcse->trdse/dot_general | solution.py:59
  1115.0 22.1 %fusion.45 = (f32[64,4,1,32,512]{4,0,2,3,1:T(8,128)}, f32[64,4,1,32,512]{4,0,2,3,1:T(8,128)}) fusion(f32[64,4,2,32,512]{4,0,2,3,1:T(8,128)} %fusion.15), kind=kLoop, calls=%fused_computation.93 | loop fusion | bytes 67108864 | tf_op jit(solution)/shard_map/slice | solution.py:68
  1137.2 22.8 %slice.43 = f32[64,4,1,32,512]{4,0,2,3,1:T(8,128)} reverse(f32[64,4,1,32,512]{4,0,2,3,1:T(8,128)} %get-tuple-element.56), dimensions={0} | reverse | bytes 33554432 | tf_op jit(solution)/shard_map/slice | solution.py:68
  1160.0 22.9 %slice.46 = f32[64,4,1,32,512]{4,0,2,3,1:T(8,128)} reverse(f32[64,4,1,32,512]{4,0,2,3,1:T(8,128)} %get-tuple-element.55), dimensions={0} | reverse | bytes 33554432 | tf_op jit(solution)/shard_map/slice | solution.py:68
  1182.8 29.6 %subtract_convert_fusion = (bf16[64,4,1,32,512]{4,0,2,3,1:T(8,128)(2,1)}, bf16[64,4,1,32,512]{4,0,2,3,1:T(8,128)(2,1)}) fusion(f32[64,4,1,32,512]{4,0,2,3,1:T(8,128)} %slice.46, f32[64,4,1,32,512]{4,0,2,3,1:T(8,128)} %slice.43, f32[64,4,2,32,512]{4,0,2,3,1:T(8,128)} %fusion.12), kind=kLoop, calls=%fused_computation.25 | loop fusion | flops 33554432 | bytes 83886080 | tf_op jit(solution)/shard_map/convert.8
  1212.4 12.1 fusion
  1224.5 24.5 %copy.62 = bf16[64,4,2,32,512]{4,2,3,1,0:T(2,128)(2,1)} copy(bf16[64,4,2,32,512]{4,0,2,3,1:T(8,128)(2,1)} %fusion) | data formatting | bytes 33554432 | tf_op jit(solution)/shard_map/convert_element_type | solution.py:97
  1249.0 5.3 all-to-all-start.2
  1254.8 361.6 %all-to-all-done.2 = bf16[64,4,2,32,512]{4,2,3,1,0:T(2,128)(2,1)} async-done(((bf16[64,4,2,32,512]{4,2,3,1,0:T(2,128)(2,1)}), bf16[64,4,2,32,512]{4,2,3,1,0:T(2,128)(2,1)}, u32[]{:S(2)}, u32[]{:S(2)}) %all-to-all-start.2) | async-done | bytes 16777248 | tf_op jit(solution)/shard_map/all_to_all | solution.py:99
  1616.4 10.6 copy.63
  1626.9 7.2 copy.64
  1634.2 23.6 %add_convert_fusion = bf16[4,4,2,512,512]{4,3,2,1,0:T(8,128)(2,1)} fusion(f32[2,512,512]{2,1,0:T(8,128)S(1)} %broadcast_multiply_fusion, bf16[4,4,2,512,512]{4,3,2,1,0:T(8,128)(2,1)} %bitcast.167, bf16[512,512]{1,0:T(8,128)(2,1)S(1)} %copy-done), kind=kOutput, calls=%fused_computation.9 | convolution fusion | flops 17205035008 | bytes 36175872 | tf_op jit(solution)/shard_map/frcij,jk->frcik/dot_general | solution.py:79
  (43 shorter events, 24.4 us)
Async XLA Ops:
  0.0 16.8 %slice-start = ((s8[16777216]{0:T(1024)(128)(4,1)}), s8[4194304]{0:T(1024)(128)(4,1)S(1)}, s32[]{:S(2)}) async-start(s8[16777216]{0:T(1024)(128)(4,1)} %bitcast.165), calls=%async_computation.3 | async-start | bytes 8388608
  0.1 16.7 %slice-start.1 = ((s8[16777216]{0:T(1024)(128)(4,1)}), s8[4194304]{0:T(1024)(128)(4,1)S(1)}, s32[]{:S(2)}) async-start(s8[16777216]{0:T(1024)(128)(4,1)} %bitcast.165), calls=%async_computation.4 | async-start | bytes 8388608
  0.1 16.7 %slice-start.2 = ((s8[16777216]{0:T(1024)(128)(4,1)}), s8[4194304]{0:T(1024)(128)(4,1)S(1)}, s32[]{:S(2)}) async-start(s8[16777216]{0:T(1024)(128)(4,1)} %bitcast.165), calls=%async_computation.5 | async-start | bytes 8388608
  0.1 16.7 %slice-start.3 = ((s8[16777216]{0:T(1024)(128)(4,1)}), s8[4194304]{0:T(1024)(128)(4,1)S(1)}, s32[]{:S(2)}) async-start(s8[16777216]{0:T(1024)(128)(4,1)} %bitcast.165), calls=%async_computation.6 | async-start | bytes 8388608
  269.5 6.9 copy-start.2
  269.5 368.9 %all-to-all-start = ((bf16[4,4,2,512,512]{4,2,1,0,3:T(2,128)(2,1)}), bf16[4,4,2,512,512]{4,2,1,0,3:T(2,128)(2,1)}, u32[]{:S(2)}, u32[]{:S(2)}) async-start(bf16[4,4,2,512,512]{4,2,1,0,3:T(2,128)(2,1)} %pad_maximum_fusion), calls=%async_computation | async-start | bytes 33554432 | tf_op jit(solution)/shard_map/all_to_all | solution.py:93
  475.6 168.1 %copy-start.1 = (s32[2,64]{1,0:T(2,128)S(1)}, s32[2,64]{1,0:T(2,128)}, u32[]{:S(2)}) copy-start(s32[2,64]{1,0:T(2,128)} %param.9) | copy-start | bytes 1540
  638.4 367.0 %all-to-all-start.1 = ((bf16[4,4,2,512,512]{4,2,1,0,3:T(2,128)(2,1)}), bf16[4,4,2,512,512]{4,2,1,0,3:T(2,128)(2,1)}, u32[]{:S(2)}, u32[]{:S(2)}) async-start(bf16[4,4,2,512,512]{4,2,1,0,3:T(2,128)(2,1)} %fusion.11), calls=%async_computation.1 | async-start | bytes 33554432 | tf_op jit(solution)/shard_map/all_to_all | solution.py:94
  1249.0 5.3 copy-start
  1249.0 367.3 %all-to-all-start.2 = ((bf16[64,4,2,32,512]{4,2,3,1,0:T(2,128)(2,1)}), bf16[64,4,2,32,512]{4,2,3,1,0:T(2,128)(2,1)}, u32[]{:S(2)}, u32[]{:S(2)}) async-start(bf16[64,4,2,32,512]{4,2,3,1,0:T(2,128)(2,1)} %copy.62), calls=%async_computation.2 | async-start | bytes 33554432 | tf_op jit(solution)/shard_map/all_to_all | solution.py:99
where the time goes:
time: 1670 us; the launch traced here: 1660 us
  waiting for transfers between devices  848 us (51%)
  local copies, waits for them, and re-layouts  450 us (27%)
  matrix products  200 us (12%)
  other arithmetic  141 us (8%)
  starting transfers between devices  17.5 us (1%)
    all_to_all x1, waiting for transfers between devices, local(): lax.all_to_all(polar_freq, 'freq', split_axis=0, concat_axis=3, tiled=True)  362 us
    all_to_all x1, waiting for transfers between devices, local(): lax.all_to_all(hole_freq, 'freq', split_axis=3, concat_axis=0, tiled=True)  324 us
    all_to_all x1, waiting for transfers between devices, local(): lax.all_to_all(green_freq, 'freq', split_axis=3, concat_axis=0, tiled=True)  163 us
    dot_general x8, matrix products, batched(): jnp.einsum('bij,bjk->bik', left_matrix, right_matrix, preferred_element_t...  126 us
    gather x40, local copies, waits for them, and re-layouts  112 us
    another operation x2, other arithmetic, newton_green(): jnp.stack([green_real, green_imag], axis=1).astype(jnp.bfloat16)  88.5 us
    another operation x2, local copies, waits for them, and re-layouts, newton_green(): jnp.stack([green_real, green_imag], axis=1).astype(jnp.bfloat16)  79.5 us
    all_to_all x3, local copies, waits for them, and re-layouts, local(): lax.all_to_all(hole_freq, 'freq', split_axis=3, concat_axis=0, tiled=True)  70.7 us
  transfers between devices with their start and end apart: 3, of which 3 were waited for; matrix products, arithmetic and copies ran while one was open for 14% of the time, Pallas kernels for 0%

commit v1 on v0

--- a/solution.py
+++ b/solution.py
@@ -1,8 +1,11 @@
+import functools
 import math
 
 import jax
 import jax.numpy as jnp
 from jax import lax
+from jax.experimental import pallas as pl
+from jax.experimental.pallas import tpu as pltpu
 from jax.sharding import PartitionSpec as P
 
 NT = 64
@@ -100,6 +103,339 @@
     )
 
 
+MESH = pl.DeviceIdType.MESH
+PEERS = 16
+TILE = 128
+HALF = 64
+PAIRS = [(0, 1), (0, 2), (0, 3), (1, 2), (1, 3), (2, 3)]
+VMEM_LIMIT = 60 * 2**20
+
+
+def dot(left, right):
+    return jnp.dot(left, right, preferred_element_type=jnp.float32)
+
+
+def greet_all(me):
+    barrier = pltpu.get_barrier_semaphore()
+    for step in range(1, PEERS):
+        peer = lax.rem(me + step, PEERS)
+        pl.semaphore_signal(barrier, inc=1, device_id={"freq": peer}, device_id_type=MESH)
+    pl.semaphore_wait(barrier, PEERS - 1)
+
+
+def green_kernel(freqs, vectors, dyson_ref, guess_ref, recv_ref, corr, green, send, send_sem, recv_sem, own_sem):
+    me = lax.axis_index("freq")
+    grid_step = pl.program_id(0)
+    steps = freqs * vectors
+    slot = lax.rem(grid_step, 2)
+
+    def copy_to(step, at_slot, at_step):
+        peer = lax.rem(me + step, PEERS)
+        return pltpu.make_async_remote_copy(
+            src_ref=send.at[at_slot, peer],
+            dst_ref=recv_ref.at[me * freqs + at_step // vectors, lax.rem(at_step, vectors)],
+            send_sem=send_sem.at[at_slot, step],
+            recv_sem=recv_sem.at[me],
+            device_id={"freq": peer},
+            device_id_type=MESH,
+        )
+
+    def copy_own(at_slot, at_step):
+        return pltpu.make_async_copy(
+            send.at[at_slot, me],
+            recv_ref.at[me * freqs + at_step // vectors, lax.rem(at_step, vectors)],
+            own_sem.at[at_slot],
+        )
+
+    def wait_slot(at_slot, at_step):
+        for step in range(1, PEERS):
+            copy_to(step, at_slot, at_step).wait_send()
+        copy_own(at_slot, at_step).wait()
+
+    @pl.when(grid_step == 0)
+    def _():
+        greet_all(me)
+
+    size = dyson_ref.shape[-1]
+    guess_real, guess_imag = guess_ref[0, 0, 0], guess_ref[0, 0, 1]
+    for row in range(0, size, 256):
+        rows = pl.ds(row, 256)
+        dyson_real, dyson_imag = dyson_ref[0, 0, 0, rows, :], dyson_ref[0, 0, 1, rows, :]
+        line = lax.broadcasted_iota(jnp.int32, (256, size), 0) + row
+        column = lax.broadcasted_iota(jnp.int32, (256, size), 1)
+        twice = jnp.where(line == column, 2.0, 0.0).astype(jnp.float32)
+        product_real = dot(dyson_real, guess_real) - dot(dyson_imag, guess_imag)
+        product_imag = dot(dyson_real, guess_imag) + dot(dyson_imag, guess_real)
+        corr[0, rows, :] = (twice - product_real).astype(jnp.bfloat16)
+        corr[1, rows, :] = (-product_imag).astype(jnp.bfloat16)
+    corr_real, corr_imag = corr[0], corr[1]
+    for row in range(0, size, 256):
+        rows = pl.ds(row, 256)
+        left_real, left_imag = guess_ref[0, 0, 0, rows, :], guess_ref[0, 0, 1, rows, :]
+        green[0, rows, :] = dot(left_real, corr_real) - dot(left_imag, corr_imag)
+        green[1, rows, :] = dot(left_real, corr_imag) + dot(left_imag, corr_real)
+
+    @pl.when(grid_step >= 2)
+    def _():
+        wait_slot(slot, grid_step - 2)
+
+    for part in range(2):
+        for index, (low, high) in enumerate(PAIRS):
+            upper = green[part, pl.ds(low * TILE, TILE), pl.ds(high * TILE, TILE)].astype(jnp.bfloat16)
+            lower = green[part, pl.ds(high * TILE, TILE), pl.ds(low * TILE, TILE)].T.astype(jnp.bfloat16)
+            for half in range(2):
+                cut = slice(half * HALF, (half + 1) * HALF)
+                send[slot, 2 * index + half, part, pl.ds(0, HALF), :] = upper[cut]
+                send[slot, 2 * index + half, part, pl.ds(HALF, HALF), :] = lower[cut]
+        for block in range(4):
+            span = pl.ds(block * TILE, TILE)
+            send[slot, 2 * len(PAIRS) + block, part] = green[part, span, span].astype(jnp.bfloat16)
+
+    for step in range(1, PEERS):
+        copy_to(step, slot, grid_step).start()
+    copy_own(slot, grid_step).start()
+
+    @pl.when(grid_step == steps - 1)
+    def _():
+        wait_slot((steps - 2) % 2, steps - 2)
+        wait_slot((steps - 1) % 2, steps - 1)
+        for step in range(1, PEERS):
+            peer = lax.rem(me + step, PEERS)
+            slab = recv_ref.at[pl.ds(peer * freqs, freqs)]
+            pltpu.make_async_remote_copy(
+                src_ref=slab,
+                dst_ref=slab,
+                send_sem=send_sem.at[0, step],
+                recv_sem=recv_sem.at[peer],
+                device_id={"freq": peer},
+                device_id_type=MESH,
+            ).wait_recv()
+
+
+def green_blocks(dyson, guess):
+    freqs, vectors, _, size, _ = dyson.shape
+    steps = freqs * vectors
+    block = pl.BlockSpec((1, 1, 2, size, size), lambda g: (g // vectors, g % vectors, 0, 0, 0))
+    return pl.pallas_call(
+        functools.partial(green_kernel, freqs, vectors),
+        out_shape=jax.ShapeDtypeStruct((freqs * PEERS, vectors, 2, TILE, TILE), jnp.bfloat16),
+        grid=(steps,),
+        in_specs=[block, block],
+        out_specs=pl.BlockSpec(memory_space=pl.ANY),
+        scratch_shapes=[
+            pltpu.VMEM((2, size, size), jnp.bfloat16),
+            pltpu.VMEM((2, size, size), jnp.float32),
+            pltpu.VMEM((2, PEERS, 2, TILE, TILE), jnp.bfloat16),
+            pltpu.SemaphoreType.DMA((2, PEERS)),
+            pltpu.SemaphoreType.DMA((PEERS,)),
+            pltpu.SemaphoreType.DMA((2,)),
+        ],
+        compiler_params=pltpu.CompilerParams(
+            collective_id=0, has_side_effects=True, vmem_limit_bytes=VMEM_LIMIT
+        ),
+    )(dyson, guess)
+
+
+def exchange_kernel(values_ref, recv_ref, send_sem, recv_sem, own_sem):
+    me = lax.axis_index("freq")
+    chunk = values_ref.shape[0] // PEERS
+    greet_all(me)
+
+    def copy_to(step):
+        peer = lax.rem(me + step, PEERS)
+        return pltpu.make_async_remote_copy(
+            src_ref=values_ref.at[pl.ds(peer * chunk, chunk)],
+            dst_ref=recv_ref.at[me],
+            send_sem=send_sem.at[step],
+            recv_sem=recv_sem.at[step],
+            device_id={"freq": peer},
+            device_id_type=MESH,
+        )
+
+    own = pltpu.make_async_copy(values_ref.at[pl.ds(me * chunk, chunk)], recv_ref.at[me], own_sem)
+    for step in range(1, PEERS):
+        copy_to(step).start()
+    own.start()
+    for step in range(1, PEERS):
+        copy_to(step).wait_send()
+    own.wait()
+    for step in range(1, PEERS):
+        source = lax.rem(me + PEERS - step, PEERS)
+        pltpu.make_async_remote_copy(
+            src_ref=recv_ref.at[source],
+            dst_ref=recv_ref.at[source],
+            send_sem=send_sem.at[step],
+            recv_sem=recv_sem.at[step],
+            device_id={"freq": source},
+            device_id_type=MESH,
+        ).wait_recv()
+
+
+def exchange(values):
+    total = values.shape[0]
+    return pl.pallas_call(
+        exchange_kernel,
+        out_shape=jax.ShapeDtypeStruct((PEERS, total // PEERS) + values.shape[1:], values.dtype),
+        in_specs=[pl.BlockSpec(memory_space=pl.ANY)],
+        out_specs=pl.BlockSpec(memory_space=pl.ANY),
+        scratch_shapes=[
+            pltpu.SemaphoreType.DMA((PEERS,)),
+            pltpu.SemaphoreType.DMA((PEERS,)),
+            pltpu.SemaphoreType.DMA,
+        ],
+        compiler_params=pltpu.CompilerParams(
+            collective_id=1, has_side_effects=True, vmem_limit_bytes=VMEM_LIMIT
+        ),
+    )(values)
+
+
+def mirror_kernel(diagonal_ref, values_ref, out_ref):
+    @pl.when(diagonal_ref[0] == 0)
+    def _():
+        out_ref[:, :, pl.ds(0, HALF), :] = values_ref[:, :, pl.ds(HALF, HALF), :]
+        out_ref[:, :, pl.ds(HALF, HALF), :] = values_ref[:, :, pl.ds(0, HALF), :]
+
+    @pl.when(diagonal_ref[0] != 0)
+    def _():
+        for row in range(values_ref.shape[0]):
+            for part in range(2):
+                out_ref[row, part] = values_ref[row, part].astype(jnp.float32).T.astype(jnp.bfloat16)
+
+
+def mirror(diagonal, values):
+    freqs, vectors, _, _, _ = values.shape
+    flat = values.reshape(freqs * vectors, 2, TILE, TILE)
+    block = pl.BlockSpec((16, 2, TILE, TILE), lambda g, flag: (g, 0, 0, 0))
+    out = pl.pallas_call(
+        mirror_kernel,
+        out_shape=jax.ShapeDtypeStruct(flat.shape, flat.dtype),
+        grid_spec=pltpu.PrefetchScalarGridSpec(
+            num_scalar_prefetch=1, grid=(flat.shape[0] // 16,), in_specs=[block], out_specs=block
+        ),
+        compiler_params=pltpu.CompilerParams(vmem_limit_bytes=VMEM_LIMIT),
+    )(diagonal, flat)
+    return out.reshape(values.shape)
+
+
+CHUNK = 16
+GROUP = 4
+
+
+def polar_kernel(partner_ref, green_ref, hole_ref, forward_ref, mirrored_ref, backward_ref, out_ref, green_wide, hole_wide, out_wide):
+    rows = green_wide.shape[0]
+    depth = rows // CHUNK
+    green_wide[...] = green_ref[...].reshape(rows, TILE).astype(jnp.float32)
+    hole_wide[...] = hole_ref[...].reshape(rows, TILE).astype(jnp.float32)
+    times = forward_ref.shape[0] // 2
+    for start in range(0, CHUNK, GROUP):
+        def gather(wide):
+            return jnp.concatenate(
+                [wide[pl.ds(start + k, depth, stride=CHUNK), :] for k in range(GROUP)], axis=1
+            ).astype(jnp.bfloat16)
+        green_time = dot(forward_ref[...], gather(green_wide))
+        hole_time = dot(mirrored_ref[...], gather(hole_wide))
+        green_real, green_imag = green_time[:times], green_time[times:]
+        hole_real, hole_imag = hole_time[:times], hole_time[times:]
+        polar_real = green_real * hole_real - green_imag * hole_imag
+        polar_imag = green_real * hole_imag + green_imag * hole_real
+        polar = jnp.concatenate([polar_real, polar_imag], axis=0).astype(jnp.bfloat16)
+        result = dot(backward_ref[...], polar)
+        for k in range(GROUP):
+            out_wide[pl.ds(start + k, result.shape[0], stride=CHUNK), :] = result[:, k * TILE:(k + 1) * TILE]
+    out_ref[...] = out_wide[...].astype(jnp.bfloat16).reshape(out_ref.shape)
+
+
+def polarization(partner, green, hole, forward, mirrored, backward):
+    freqs, vectors, _, _, _ = green.shape
+    outs = backward.shape[0] // 2
+    table = pl.BlockSpec(forward.shape, lambda r, k, p: (0, 0))
+    back_table = pl.BlockSpec(backward.shape, lambda r, k, p: (0, 0))
+    return pl.pallas_call(
+        polar_kernel,
+        out_shape=jax.ShapeDtypeStruct((outs, vectors, 2, TILE, TILE), jnp.bfloat16),
+        grid_spec=pltpu.PrefetchScalarGridSpec(
+            num_scalar_prefetch=1,
+            grid=(vectors, TILE // CHUNK),
+            in_specs=[
+                pl.BlockSpec((freqs, 1, 2, CHUNK, TILE), lambda r, k, p: (0, r, 0, k, 0)),
+                pl.BlockSpec((freqs, 1, 2, CHUNK, TILE), lambda r, k, p: (0, p[r], 0, k, 0)),
+                table, table, back_table,
+            ],
+            out_specs=pl.BlockSpec((outs, 1, 2, CHUNK, TILE), lambda r, k, p: (0, r, 0, k, 0)),
+            scratch_shapes=[
+                pltpu.VMEM((freqs * 2 * CHUNK, TILE), jnp.float32),
+                pltpu.VMEM((freqs * 2 * CHUNK, TILE), jnp.float32),
+                pltpu.VMEM((outs * 2 * CHUNK, TILE), jnp.float32),
+            ],
+        ),
+        compiler_params=pltpu.CompilerParams(vmem_limit_bytes=VMEM_LIMIT),
+    )(partner, green, hole, forward, mirrored, backward)
+
+
+def screen_kernel(blocks_ref, coulomb_ref, out_ref, polar, mixed):
+    for part in range(2):
+        for index, (low, high) in enumerate(PAIRS):
+            upper = [blocks_ref[2 * index + half, 0, 0, part, pl.ds(0, HALF), :] for half in range(2)]
+            lower = [blocks_ref[2 * index + half, 0, 0, part, pl.ds(HALF, HALF), :] for half in range(2)]
+            for half in range(2):
+                polar[part, pl.ds(low * TILE + half * HALF, HALF), pl.ds(high * TILE, TILE)] = upper[half]
+            turned = jnp.concatenate(lower, axis=0).astype(jnp.float32).T.astype(jnp.bfloat16)
+            polar[part, pl.ds(high * TILE, TILE), pl.ds(low * TILE, TILE)] = turned
+        for block in range(4):
+            span = pl.ds(block * TILE, TILE)
+            polar[part, span, span] = blocks_ref[2 * len(PAIRS) + block, 0, 0, part]
+    size = coulomb_ref.shape[0]
+    for part in range(2):
+        for row in range(0, size, 256):
+            rows = pl.ds(row, 256)
+            mixed[rows, :] = dot(coulomb_ref[rows, :], polar[part]).astype(jnp.bfloat16)
+        for row in range(0, size, 256):
+            rows = pl.ds(row, 256)
+            product = dot(mixed[rows, :], coulomb_ref[...])
+            if part == 0:
+                product = product + coulomb_ref[rows, :].astype(jnp.float32)
+            out_ref[0, 0, part, rows, :] = product.astype(jnp.bfloat16)
+
+
+def screen_blocks(blocks, coulomb):
+    _, freqs, vectors, _, _, _ = blocks.shape
+    size = coulomb.shape[0]
+    return pl.pallas_call(
+        screen_kernel,
+        out_shape=jax.ShapeDtypeStruct((freqs, vectors, 2, size, size), jnp.bfloat16),
+        grid=(freqs, vectors),
+        in_specs=[
+            pl.BlockSpec((PEERS, 1, 1, 2, TILE, TILE), lambda v, r: (0, v, r, 0, 0, 0)),
+            pl.BlockSpec((size, size), lambda v, r: (0, 0)),
+        ],
+        out_specs=pl.BlockSpec((1, 1, 2, size, size), lambda v, r: (v, r, 0, 0, 0)),
+        scratch_shapes=[
+            pltpu.VMEM((2, size, size), jnp.bfloat16),
+            pltpu.VMEM((size, size), jnp.bfloat16),
+        ],
+        compiler_params=pltpu.CompilerParams(vmem_limit_bytes=VMEM_LIMIT),
+    )(blocks, coulomb)
+
+
+def tables(freq_index):
+    forward = fermion_table(freq_index, NT)
+    backward = boson_table(freq_index, NT)
+    freqs = forward.shape[2]
+    plain = jnp.transpose(forward, (1, 0, 2, 3)).reshape(2 * NT, 2 * freqs)
+    mirrored = jnp.transpose(forward[::-1], (1, 0, 2, 3)).reshape(2 * NT, 2 * freqs)
+    back = jnp.transpose(backward, (0, 1, 3, 2)).reshape(2 * freqs, 2 * NT)
+    return plain, mirrored, back
+
+
+def local_paired(dyson, guess, coulomb, partner, freq_index):
+    forward, mirrored, backward = tables(freq_index)
+    diagonal = (lax.axis_index("freq") >= 2 * len(PAIRS)).astype(jnp.int32).reshape(1)
+    green = green_blocks(dyson, guess)
+    hole = mirror(diagonal, green)
+    polar = polarization(partner, green, hole, forward, mirrored, backward)
+    return screen_blocks(exchange(polar), coulomb)
+
+
 def solution(mesh):
     in_specs = (
         P(("groups", "freq"), None, None, None, None),
@@ -109,4 +445,5 @@
         P(),
     )
     out_specs = P(("groups", "freq"), None, None, None, None)
-    return jax.shard_map(local, mesh=mesh, in_specs=in_specs, out_specs=out_specs, check_vma=False)
+    body = local_paired if mesh.shape["freq"] == PEERS else local
+    return jax.shard_map(body, mesh=mesh, in_specs=in_specs, out_specs=out_specs, check_vma=False)

time: 1670 us -> 843 us (0.50)
  waiting for transfers between devices: 848 us -> 0 us
  Pallas kernels: 0 us -> 838 us
  local copies, waits for them, and re-layouts: 450 us -> 2.63 us
  matrix products: 200 us -> 0 us
  other arithmetic: 141 us -> 1.17 us
  starting transfers between devices: 17.5 us -> 0 us
    all_to_all x3 -> x0, waiting for transfers between devices: 848 us -> none  [the longest x1 362 us: local(): lax.all_to_all(polar_freq, 'freq', split_axis=0, concat_axis=3, tiled=True)]
    pallas_call x0 -> x5, Pallas kernels: none -> 838 us  [the longest x1 370 us: green_blocks(): pl.pallas_call(functools.partial(green_kernel, freqs, vectors), out_shape...]
    dot_general x12 -> x0, matrix products: 200 us -> none  [the longest x8 126 us: batched(): jnp.einsum('bij,bjk->bik', left_matrix, right_matrix, preferred_element_t...]
    all_to_all x7 -> x0, local copies, waits for them, and re-layouts: 126 us -> none  [the longest x3 70.7 us: local(): lax.all_to_all(hole_freq, 'freq', split_axis=3, concat_axis=0, tiled=True)]
    another operation x5 -> x1, other arithmetic: 119 us -> 0.35 us  [the longest x2 88.5 us: newton_green(): jnp.stack([green_real, green_imag], axis=1).astype(jnp.bfloat16)]
    gather x40 -> x0, local copies, waits for them, and re-layouts: 112 us -> none
    another operation x2 -> x0, local copies, waits for them, and re-layouts: 79.5 us -> none  [newton_green(): jnp.stack([green_real, green_imag], axis=1).astype(jnp.bfloat16)]
    slice x3 -> x0, local copies, waits for them, and re-layouts: 67.8 us -> none  [polarize(): hole_real, hole_imag = (hole_time[:, :, 0], hole_time[:, :, 1])]
  transfers between devices with their start and end apart: 3 -> 0, of which waited for: 3 -> 0; matrix products, arithmetic and copies ran while one was open for 14% -> 0% of each run, Pallas kernels for 0% -> 0%
where the time goes in v1:
time: 843 us; the launch traced here: 842 us
  Pallas kernels  838 us (99%)
    pallas_call x1, Pallas kernels, green_blocks(): pl.pallas_call(functools.partial(green_kernel, freqs, vectors), out_shape...  370 us
    pallas_call x1, Pallas kernels, exchange(): pl.pallas_call(exchange_kernel, out_shape=jax.ShapeDtypeStruct((PEERS, to...  366 us
    pallas_call x1, Pallas kernels, polarization(): pl.pallas_call(polar_kernel, out_shape=jax.ShapeDtypeStruct((outs, vector...  58 us
    pallas_call x1, Pallas kernels, screen_blocks(): pl.pallas_call(screen_kernel, out_shape=jax.ShapeDtypeStruct((freqs, vect...  26.4 us
    pallas_call x1, Pallas kernels, mirror(): pl.pallas_call(mirror_kernel, out_shape=jax.ShapeDtypeStruct(flat.shape,...  17.5 us

profile of v1, /device:TPU:13, one launch (start us, length us, event | category | flops | bytes accessed | tf_op | source)
XLA Modules:
  0.0 841.6 jit_solution(12638921336486293183)
XLA Ops:
  0.0 0.8 slice_bitcast_fusion
  0.8 0.4 negate_convert_fusion
  1.2 0.1 copy.15
  1.3 0.7 reshape.427.backward_ref
  2.0 0.1 copy.14
  2.1 0.1 reshape.426
  2.2 0.7 copy.17.mirrored_ref
  2.9 0.1 copy.13
  3.0 0.1 reshape.425
  3.1 0.7 copy.16.forward_ref
  3.9 369.6 %shard_map.55.green_ref = bf16[64,4,2,128,128]{4,3,2,1,0:T(8,128)(2,1)} custom-call(bf16[4,4,2,512,512]{4,3,2,1,0:T(8,128)(2,1)} %dyson_ref.1, bf16[4,4,2,512,512]{4,3,2,1,0:T(8,128)(2,1)} %guess_ref.1), custom_call_target="tpu_custom_call" | custom-call | tf_op jit(solution)/shard_map/pallas_call | solution.py:219
  373.5 17.5 %shard_map.56 = bf16[256,2,128,128]{3,2,1,0:T(8,128)(2,1)} custom-call(s32[1]{0:T(128)} %bitcast.diagonal_ref, bf16[256,2,128,128]{3,2,1,0:T(8,128)(2,1)} %bitcast.24), custom_call_target="tpu_custom_call" | custom-call | tf_op jit(solution)/shard_map/pallas_call | solution.py:309
  391.0 58.0 %shard_map.57.values_ref = bf16[64,4,2,128,128]{4,3,2,1,0:T(8,128)(2,1)} custom-call(s32[4]{0:T(128)} %partner_ref.1, bf16[64,4,2,128,128]{4,3,2,1,0:T(8,128)(2,1)} %shard_map.55.green_ref, bf16[64,4,2,128,128]{4,3,2,1,0:T(8,128)(2,1)} %bitcast.25, bf16[128,128]{1,0:T(8,128)(2,1)} %copy.16.forward_ref, bf16[128,128]{1,0:T(8,128)(2,1)} %copy.17.mirrored_ref, ...), custom_call_target="tpu_custom_call" | custom-call | tf_op jit(solution)/shard_map/pallas_call | solution.py:353
  448.9 366.2 %shard_map.58.blocks_ref = bf16[16,4,4,2,128,128]{5,4,3,2,1,0:T(8,128)(2,1)} custom-call(bf16[64,4,2,128,128]{4,3,2,1,0:T(8,128)(2,1)} %shard_map.57.values_ref), custom_call_target="tpu_custom_call" | custom-call | tf_op jit(solution)/shard_map/pallas_call | solution.py:276
  815.2 26.4 %shard_map.59 = bf16[4,4,2,512,512]{4,3,2,1,0:T(8,128)(2,1)} custom-call(bf16[16,4,4,2,128,128]{5,4,3,2,1,0:T(8,128)(2,1)} %shard_map.58.blocks_ref, bf16[512,512]{1,0:T(8,128)(2,1)} %coulomb_ref.1), custom_call_target="tpu_custom_call" | custom-call | tf_op jit(solution)/shard_map/pallas_call | solution.py:403
  (5 shorter events, 0.1 us)

commit v2 on v1

--- a/solution.py
+++ b/solution.py
@@ -123,34 +123,29 @@
     pl.semaphore_wait(barrier, PEERS - 1)
 
 
+def peer_at(me, step):
+    half = PEERS // 2
+    side = me // half
+    if step < half:
+        return (1 - side) * half + lax.rem(me + step, half)
+    return side * half + lax.rem(me + step - half + 1, half)
+
+
 def green_kernel(freqs, vectors, dyson_ref, guess_ref, recv_ref, corr, green, send, send_sem, recv_sem, own_sem):
     me = lax.axis_index("freq")
     grid_step = pl.program_id(0)
     steps = freqs * vectors
-    slot = lax.rem(grid_step, 2)
-
-    def copy_to(step, at_slot, at_step):
-        peer = lax.rem(me + step, PEERS)
+    freq, vector = grid_step // vectors, lax.rem(grid_step, vectors)
+
+    def remote(step, source, target):
         return pltpu.make_async_remote_copy(
-            src_ref=send.at[at_slot, peer],
-            dst_ref=recv_ref.at[me * freqs + at_step // vectors, lax.rem(at_step, vectors)],
-            send_sem=send_sem.at[at_slot, step],
+            src_ref=source,
+            dst_ref=target,
+            send_sem=send_sem.at[step],
             recv_sem=recv_sem.at[me],
-            device_id={"freq": peer},
+            device_id={"freq": peer_at(me, step)},
             device_id_type=MESH,
         )
-
-    def copy_own(at_slot, at_step):
-        return pltpu.make_async_copy(
-            send.at[at_slot, me],
-            recv_ref.at[me * freqs + at_step // vectors, lax.rem(at_step, vectors)],
-            own_sem.at[at_slot],
-        )
-
-    def wait_slot(at_slot, at_step):
-        for step in range(1, PEERS):
-            copy_to(step, at_slot, at_step).wait_send()
-        copy_own(at_slot, at_step).wait()
 
     @pl.when(grid_step == 0)
     def _():
@@ -175,37 +170,35 @@
         green[0, rows, :] = dot(left_real, corr_real) - dot(left_imag, corr_imag)
         green[1, rows, :] = dot(left_real, corr_imag) + dot(left_imag, corr_real)
 
-    @pl.when(grid_step >= 2)
-    def _():
-        wait_slot(slot, grid_step - 2)
-
     for part in range(2):
         for index, (low, high) in enumerate(PAIRS):
             upper = green[part, pl.ds(low * TILE, TILE), pl.ds(high * TILE, TILE)].astype(jnp.bfloat16)
             lower = green[part, pl.ds(high * TILE, TILE), pl.ds(low * TILE, TILE)].T.astype(jnp.bfloat16)
             for half in range(2):
                 cut = slice(half * HALF, (half + 1) * HALF)
-                send[slot, 2 * index + half, part, pl.ds(0, HALF), :] = upper[cut]
-                send[slot, 2 * index + half, part, pl.ds(HALF, HALF), :] = lower[cut]
+                send[freq, vector, 2 * index + half, part, pl.ds(0, HALF), :] = upper[cut]
+                send[freq, vector, 2 * index + half, part, pl.ds(HALF, HALF), :] = lower[cut]
         for block in range(4):
             span = pl.ds(block * TILE, TILE)
-            send[slot, 2 * len(PAIRS) + block, part] = green[part, span, span].astype(jnp.bfloat16)
-
-    for step in range(1, PEERS):
-        copy_to(step, slot, grid_step).start()
-    copy_own(slot, grid_step).start()
+            send[freq, vector, 2 * len(PAIRS) + block, part] = green[part, span, span].astype(jnp.bfloat16)
+
+    for step in range(PEERS - 1):
+        remote(step, send.at[freq, vector, peer_at(me, step)], recv_ref.at[me * freqs + freq, vector]).start()
+    pltpu.make_async_copy(send.at[freq, vector, me], recv_ref.at[me * freqs + freq, vector], own_sem).start()
 
     @pl.when(grid_step == steps - 1)
     def _():
-        wait_slot((steps - 2) % 2, steps - 2)
-        wait_slot((steps - 1) % 2, steps - 1)
-        for step in range(1, PEERS):
-            peer = lax.rem(me + step, PEERS)
+        own_slab = recv_ref.at[pl.ds(me * freqs, freqs)]
+        for step in range(PEERS - 1):
+            remote(step, send.at[:, :, peer_at(me, step)], own_slab).wait_send()
+        pltpu.make_async_copy(send.at[:, :, me], own_slab, own_sem).wait()
+        for step in range(PEERS - 1):
+            peer = peer_at(me, step)
             slab = recv_ref.at[pl.ds(peer * freqs, freqs)]
             pltpu.make_async_remote_copy(
                 src_ref=slab,
                 dst_ref=slab,
-                send_sem=send_sem.at[0, step],
+                send_sem=send_sem.at[step],
                 recv_sem=recv_sem.at[peer],
                 device_id={"freq": peer},
                 device_id_type=MESH,
@@ -225,68 +218,15 @@
         scratch_shapes=[
             pltpu.VMEM((2, size, size), jnp.bfloat16),
             pltpu.VMEM((2, size, size), jnp.float32),
-            pltpu.VMEM((2, PEERS, 2, TILE, TILE), jnp.bfloat16),
-            pltpu.SemaphoreType.DMA((2, PEERS)),
+            pltpu.VMEM((freqs, vectors, PEERS, 2, TILE, TILE), jnp.bfloat16),
+            pltpu.SemaphoreType.DMA((PEERS - 1,)),
             pltpu.SemaphoreType.DMA((PEERS,)),
-            pltpu.SemaphoreType.DMA((2,)),
+            pltpu.SemaphoreType.DMA,
         ],
         compiler_params=pltpu.CompilerParams(
             collective_id=0, has_side_effects=True, vmem_limit_bytes=VMEM_LIMIT
         ),
     )(dyson, guess)
-
-
-def exchange_kernel(values_ref, recv_ref, send_sem, recv_sem, own_sem):
-    me = lax.axis_index("freq")
-    chunk = values_ref.shape[0] // PEERS
-    greet_all(me)
-
-    def copy_to(step):
-        peer = lax.rem(me + step, PEERS)
-        return pltpu.make_async_remote_copy(
-            src_ref=values_ref.at[pl.ds(peer * chunk, chunk)],
-            dst_ref=recv_ref.at[me],
-            send_sem=send_sem.at[step],
-            recv_sem=recv_sem.at[step],
-            device_id={"freq": peer},
-            device_id_type=MESH,
-        )
-
-    own = pltpu.make_async_copy(values_ref.at[pl.ds(me * chunk, chunk)], recv_ref.at[me], own_sem)
-    for step in range(1, PEERS):
-        copy_to(step).start()
-    own.start()
-    for step in range(1, PEERS):
-        copy_to(step).wait_send()
-    own.wait()
-    for step in range(1, PEERS):
-        source = lax.rem(me + PEERS - step, PEERS)
-        pltpu.make_async_remote_copy(
-            src_ref=recv_ref.at[source],
-            dst_ref=recv_ref.at[source],
-            send_sem=send_sem.at[step],
-            recv_sem=recv_sem.at[step],
-            device_id={"freq": source},
-            device_id_type=MESH,
-        ).wait_recv()
-
-
-def exchange(values):
-    total = values.shape[0]
-    return pl.pallas_call(
-        exchange_kernel,
-        out_shape=jax.ShapeDtypeStruct((PEERS, total // PEERS) + values.shape[1:], values.dtype),
-        in_specs=[pl.BlockSpec(memory_space=pl.ANY)],
-        out_specs=pl.BlockSpec(memory_space=pl.ANY),
-        scratch_shapes=[
-            pltpu.SemaphoreType.DMA((PEERS,)),
-            pltpu.SemaphoreType.DMA((PEERS,)),
-            pltpu.SemaphoreType.DMA,
-        ],
-        compiler_params=pltpu.CompilerParams(
-            collective_id=1, has_side_effects=True, vmem_limit_bytes=VMEM_LIMIT
-        ),
-    )(values)
 
 
 def mirror_kernel(diagonal_ref, values_ref, out_ref):
@@ -321,11 +261,32 @@
 GROUP = 4
 
 
-def polar_kernel(partner_ref, green_ref, hole_ref, forward_ref, mirrored_ref, backward_ref, out_ref, green_wide, hole_wide, out_wide):
+def polar_kernel(
+    partner_ref, green_ref, hole_ref, forward_ref, mirrored_ref, backward_ref, recv_ref,
+    green_wide, hole_wide, out_wide, send, send_sem, recv_sem, own_sem,
+):
+    me = lax.axis_index("freq")
+    chunk, vector = pl.program_id(0), pl.program_id(1)
+    share = send.shape[2] // PEERS
+
+    def remote(step, source, target):
+        return pltpu.make_async_remote_copy(
+            src_ref=source,
+            dst_ref=target,
+            send_sem=send_sem.at[step],
+            recv_sem=recv_sem.at[me],
+            device_id={"freq": peer_at(me, step)},
+            device_id_type=MESH,
+        )
+
+    @pl.when((chunk == 0) & (vector == 0))
+    def _():
+        greet_all(me)
+
     rows = green_wide.shape[0]
     depth = rows // CHUNK
     green_wide[...] = green_ref[...].reshape(rows, TILE).astype(jnp.float32)
-    hole_wide[...] = hole_ref[...].reshape(rows, TILE).astype(jnp.float32)
+    hole_wide[...] = hole_ref[:, partner_ref[vector]].reshape(rows, TILE).astype(jnp.float32)
     times = forward_ref.shape[0] // 2
     for start in range(0, CHUNK, GROUP):
         def gather(wide):
@@ -342,48 +303,83 @@
         result = dot(backward_ref[...], polar)
         for k in range(GROUP):
             out_wide[pl.ds(start + k, result.shape[0], stride=CHUNK), :] = result[:, k * TILE:(k + 1) * TILE]
-    out_ref[...] = out_wide[...].astype(jnp.bfloat16).reshape(out_ref.shape)
+    send[chunk, vector] = out_wide[...].astype(jnp.bfloat16).reshape(send.shape[2:])
+    for step in range(PEERS - 1):
+        part = pl.ds(peer_at(me, step) * share, share)
+        remote(step, send.at[chunk, vector, part], recv_ref.at[me, chunk, vector]).start()
+    own = pl.ds(me * share, share)
+    pltpu.make_async_copy(send.at[chunk, vector, own], recv_ref.at[me, chunk, vector], own_sem).start()
+
+    @pl.when((chunk == pl.num_programs(0) - 1) & (vector == pl.num_programs(1) - 1))
+    def _():
+        for step in range(PEERS - 1):
+            part = pl.ds(peer_at(me, step) * share, share)
+            remote(step, send.at[:, :, part], recv_ref.at[me]).wait_send()
+        pltpu.make_async_copy(send.at[:, :, own], recv_ref.at[me], own_sem).wait()
+        for step in range(PEERS - 1):
+            peer = peer_at(me, step)
+            pltpu.make_async_remote_copy(
+                src_ref=recv_ref.at[peer],
+                dst_ref=recv_ref.at[peer],
+                send_sem=send_sem.at[step],
+                recv_sem=recv_sem.at[peer],
+                device_id={"freq": peer},
+                device_id_type=MESH,
+            ).wait_recv()
 
 
 def polarization(partner, green, hole, forward, mirrored, backward):
     freqs, vectors, _, _, _ = green.shape
     outs = backward.shape[0] // 2
-    table = pl.BlockSpec(forward.shape, lambda r, k, p: (0, 0))
-    back_table = pl.BlockSpec(backward.shape, lambda r, k, p: (0, 0))
+    chunks = TILE // CHUNK
     return pl.pallas_call(
         polar_kernel,
-        out_shape=jax.ShapeDtypeStruct((outs, vectors, 2, TILE, TILE), jnp.bfloat16),
-        grid_spec=pltpu.PrefetchScalarGridSpec(
-            num_scalar_prefetch=1,
-            grid=(vectors, TILE // CHUNK),
-            in_specs=[
-                pl.BlockSpec((freqs, 1, 2, CHUNK, TILE), lambda r, k, p: (0, r, 0, k, 0)),
-                pl.BlockSpec((freqs, 1, 2, CHUNK, TILE), lambda r, k, p: (0, p[r], 0, k, 0)),
-                table, table, back_table,
-            ],
-            out_specs=pl.BlockSpec((outs, 1, 2, CHUNK, TILE), lambda r, k, p: (0, r, 0, k, 0)),
-            scratch_shapes=[
-                pltpu.VMEM((freqs * 2 * CHUNK, TILE), jnp.float32),
-                pltpu.VMEM((freqs * 2 * CHUNK, TILE), jnp.float32),
-                pltpu.VMEM((outs * 2 * CHUNK, TILE), jnp.float32),
-            ],
+        out_shape=jax.ShapeDtypeStruct(
+            (PEERS, chunks, vectors, outs // PEERS, 2, CHUNK, TILE), jnp.bfloat16
         ),
-        compiler_params=pltpu.CompilerParams(vmem_limit_bytes=VMEM_LIMIT),
+        grid=(chunks, vectors),
+        in_specs=[
+            pl.BlockSpec(memory_space=pltpu.SMEM),
+            pl.BlockSpec((freqs, 1, 2, CHUNK, TILE), lambda k, r: (0, r, 0, k, 0)),
+            pl.BlockSpec((freqs, vectors, 2, CHUNK, TILE), lambda k, r: (0, 0, 0, k, 0)),
+            pl.BlockSpec(forward.shape, lambda k, r: (0, 0)),
+            pl.BlockSpec(forward.shape, lambda k, r: (0, 0)),
+            pl.BlockSpec(backward.shape, lambda k, r: (0, 0)),
+        ],
+        out_specs=pl.BlockSpec(memory_space=pl.ANY),
+        scratch_shapes=[
+            pltpu.VMEM((freqs * 2 * CHUNK, TILE), jnp.float32),
+            pltpu.VMEM((freqs * 2 * CHUNK, TILE), jnp.float32),
+            pltpu.VMEM((outs * 2 * CHUNK, TILE), jnp.float32),
+            pltpu.VMEM((chunks, vectors, outs, 2, CHUNK, TILE), jnp.bfloat16),
+            pltpu.SemaphoreType.DMA((PEERS - 1,)),
+            pltpu.SemaphoreType.DMA((PEERS,)),
+            pltpu.SemaphoreType.DMA,
+        ],
+        compiler_params=pltpu.CompilerParams(
+            collective_id=1, has_side_effects=True, vmem_limit_bytes=VMEM_LIMIT
+        ),
     )(partner, green, hole, forward, mirrored, backward)
 
 
 def screen_kernel(blocks_ref, coulomb_ref, out_ref, polar, mixed):
+    chunks = blocks_ref.shape[1]
+    mid = chunks // 2
+
+    def rows_of(source, part, start, count):
+        return blocks_ref[source, pl.ds(start, count), 0, 0, part].reshape(count * CHUNK, TILE)
+
     for part in range(2):
         for index, (low, high) in enumerate(PAIRS):
-            upper = [blocks_ref[2 * index + half, 0, 0, part, pl.ds(0, HALF), :] for half in range(2)]
-            lower = [blocks_ref[2 * index + half, 0, 0, part, pl.ds(HALF, HALF), :] for half in range(2)]
+            upper = [rows_of(2 * index + half, part, 0, mid) for half in range(2)]
+            lower = [rows_of(2 * index + half, part, mid, mid) for half in range(2)]
             for half in range(2):
                 polar[part, pl.ds(low * TILE + half * HALF, HALF), pl.ds(high * TILE, TILE)] = upper[half]
             turned = jnp.concatenate(lower, axis=0).astype(jnp.float32).T.astype(jnp.bfloat16)
             polar[part, pl.ds(high * TILE, TILE), pl.ds(low * TILE, TILE)] = turned
         for block in range(4):
             span = pl.ds(block * TILE, TILE)
-            polar[part, span, span] = blocks_ref[2 * len(PAIRS) + block, 0, 0, part]
+            polar[part, span, span] = rows_of(2 * len(PAIRS) + block, part, 0, chunks)
     size = coulomb_ref.shape[0]
     for part in range(2):
         for row in range(0, size, 256):
@@ -398,14 +394,14 @@
 
 
 def screen_blocks(blocks, coulomb):
-    _, freqs, vectors, _, _, _ = blocks.shape
+    _, chunks, vectors, freqs, _, _, _ = blocks.shape
     size = coulomb.shape[0]
     return pl.pallas_call(
         screen_kernel,
         out_shape=jax.ShapeDtypeStruct((freqs, vectors, 2, size, size), jnp.bfloat16),
         grid=(freqs, vectors),
         in_specs=[
-            pl.BlockSpec((PEERS, 1, 1, 2, TILE, TILE), lambda v, r: (0, v, r, 0, 0, 0)),
+            pl.BlockSpec((PEERS, chunks, 1, 1, 2, CHUNK, TILE), lambda v, r: (0, 0, r, v, 0, 0, 0)),
             pl.BlockSpec((size, size), lambda v, r: (0, 0)),
         ],
         out_specs=pl.BlockSpec((1, 1, 2, size, size), lambda v, r: (v, r, 0, 0, 0)),
@@ -433,7 +429,7 @@
     green = green_blocks(dyson, guess)
     hole = mirror(diagonal, green)
     polar = polarization(partner, green, hole, forward, mirrored, backward)
-    return screen_blocks(exchange(polar), coulomb)
+    return screen_blocks(polar, coulomb)
 
 
 def solution(mesh):

time: 843 us -> 796 us (0.944)
  Pallas kernels: 838 us -> 788 us
    pallas_call x2 -> x1, Pallas kernels: 424 us -> 372 us  [polarization(): pl.pallas_call(polar_kernel, out_shape=jax.ShapeDtypeStruct((PEERS, chunk...]
where the time goes in v2:
time: 796 us; the launch traced here: 792 us
  Pallas kernels  788 us (99%)
    pallas_call x1, Pallas kernels, green_blocks(): pl.pallas_call(functools.partial(green_kernel, freqs, vectors), out_shape...  373 us
    pallas_call x1, Pallas kernels, polarization(): pl.pallas_call(polar_kernel, out_shape=jax.ShapeDtypeStruct((PEERS, chunk...  372 us
    pallas_call x1, Pallas kernels, screen_blocks(): pl.pallas_call(screen_kernel, out_shape=jax.ShapeDtypeStruct((freqs, vect...  26.5 us
    pallas_call x1, Pallas kernels, mirror(): pl.pallas_call(mirror_kernel, out_shape=jax.ShapeDtypeStruct(flat.shape,...  17.5 us

profile of v2, /device:TPU:13, one launch (start us, length us, event | category | flops | bytes accessed | tf_op | source)
XLA Modules:
  0.0 792.1 jit_solution(16859561283538772826)
XLA Ops:
  0.0 0.8 slice_bitcast_fusion
  0.8 0.4 negate_convert_fusion
  1.2 0.1 copy.15
  1.3 0.7 reshape.427.backward_ref
  2.0 0.1 copy.14
  2.1 0.1 reshape.426
  2.2 0.7 copy.17.mirrored_ref
  2.9 0.1 copy.13
  3.0 0.1 reshape.425
  3.1 0.7 copy.16.forward_ref
  3.9 372.6 %shard_map.55.green_ref = bf16[64,4,2,128,128]{4,3,2,1,0:T(8,128)(2,1)} custom-call(bf16[4,4,2,512,512]{4,3,2,1,0:T(8,128)(2,1)} %dyson_ref.1, bf16[4,4,2,512,512]{4,3,2,1,0:T(8,128)(2,1)} %guess_ref.1), custom_call_target="tpu_custom_call" | custom-call | tf_op jit(solution)/shard_map/pallas_call | solution.py:212
  376.5 17.5 %shard_map.56 = bf16[256,2,128,128]{3,2,1,0:T(8,128)(2,1)} custom-call(s32[1]{0:T(128)} %bitcast.diagonal_ref, bf16[256,2,128,128]{3,2,1,0:T(8,128)(2,1)} %bitcast.24), custom_call_target="tpu_custom_call" | custom-call | tf_op jit(solution)/shard_map/pallas_call | solution.py:249
  394.0 371.6 %shard_map.57.blocks_ref = bf16[16,8,4,4,2,16,128]{6,5,4,3,2,1,0:T(8,128)(2,1)} custom-call(s32[4]{0:T(128)} %partner_ref.1, bf16[64,4,2,128,128]{4,3,2,1,0:T(8,128)(2,1)} %shard_map.55.green_ref, bf16[64,4,2,128,128]{4,3,2,1,0:T(8,128)(2,1)} %bitcast.25, bf16[128,128]{1,0:T(8,128)(2,1)} %copy.16.forward_ref, bf16[128,128]{1,0:T(8,128)(2,1)} %copy.17.mirrored_ref, ...), custom_call_target="tpu_custom_call" | custom-call | tf_op jit(solution)/shard_map/pallas_call | solution.py:335
  765.5 26.5 %shard_map.58 = bf16[4,4,2,512,512]{4,3,2,1,0:T(8,128)(2,1)} custom-call(bf16[16,8,4,4,2,16,128]{6,5,4,3,2,1,0:T(8,128)(2,1)} %shard_map.57.blocks_ref, bf16[512,512]{1,0:T(8,128)(2,1)} %coulomb_ref.1), custom_call_target="tpu_custom_call" | custom-call | tf_op jit(solution)/shard_map/pallas_call | solution.py:399
  (5 shorter events, 0.1 us)

commit v3 on v2

--- a/solution.py
+++ b/solution.py
@@ -245,12 +245,12 @@
 def mirror(diagonal, values):
     freqs, vectors, _, _, _ = values.shape
     flat = values.reshape(freqs * vectors, 2, TILE, TILE)
-    block = pl.BlockSpec((16, 2, TILE, TILE), lambda g, flag: (g, 0, 0, 0))
+    block = pl.BlockSpec((32, 2, TILE, TILE), lambda g, flag: (g, 0, 0, 0))
     out = pl.pallas_call(
         mirror_kernel,
         out_shape=jax.ShapeDtypeStruct(flat.shape, flat.dtype),
         grid_spec=pltpu.PrefetchScalarGridSpec(
-            num_scalar_prefetch=1, grid=(flat.shape[0] // 16,), in_specs=[block], out_specs=block
+            num_scalar_prefetch=1, grid=(flat.shape[0] // 32,), in_specs=[block], out_specs=block
         ),
         compiler_params=pltpu.CompilerParams(vmem_limit_bytes=VMEM_LIMIT),
     )(diagonal, flat)

time: 796 us -> 792 us (level)
  no operation moved by 1% of the time
where the time goes in v3:
time: 792 us; the launch traced here: 788 us
  Pallas kernels  785 us (99%)
    pallas_call x1, Pallas kernels, green_blocks(): pl.pallas_call(functools.partial(green_kernel, freqs, vectors), out_shape...  373 us
    pallas_call x1, Pallas kernels, polarization(): pl.pallas_call(polar_kernel, out_shape=jax.ShapeDtypeStruct((PEERS, chunk...  372 us
    pallas_call x1, Pallas kernels, screen_blocks(): pl.pallas_call(screen_kernel, out_shape=jax.ShapeDtypeStruct((freqs, vect...  26.5 us

profile of v3, /device:TPU:13, one launch (start us, length us, event | category | flops | bytes accessed | tf_op | source)
XLA Modules:
  0.0 788.4 jit_solution(9677536117154544142)
XLA Ops:
  0.0 0.8 slice_bitcast_fusion
  0.8 0.4 negate_convert_fusion
  1.2 0.1 copy.15
  1.3 0.7 reshape.427.backward_ref
  2.0 0.1 copy.14
  2.1 0.1 reshape.426
  2.2 0.7 copy.17.mirrored_ref
  2.9 0.1 copy.13
  3.0 0.1 reshape.425
  3.1 0.7 copy.16.forward_ref
  3.9 372.6 %shard_map.55.green_ref = bf16[64,4,2,128,128]{4,3,2,1,0:T(8,128)(2,1)} custom-call(bf16[4,4,2,512,512]{4,3,2,1,0:T(8,128)(2,1)} %dyson_ref.1, bf16[4,4,2,512,512]{4,3,2,1,0:T(8,128)(2,1)} %guess_ref.1), custom_call_target="tpu_custom_call" | custom-call | tf_op jit(solution)/shard_map/pallas_call | solution.py:212
  376.5 13.8 %shard_map.56 = bf16[256,2,128,128]{3,2,1,0:T(8,128)(2,1)} custom-call(s32[1]{0:T(128)} %bitcast.diagonal_ref, bf16[256,2,128,128]{3,2,1,0:T(8,128)(2,1)} %bitcast.24), custom_call_target="tpu_custom_call" | custom-call | tf_op jit(solution)/shard_map/pallas_call | solution.py:249
  390.3 371.6 %shard_map.57.blocks_ref = bf16[16,8,4,4,2,16,128]{6,5,4,3,2,1,0:T(8,128)(2,1)} custom-call(s32[4]{0:T(128)} %partner_ref.1, bf16[64,4,2,128,128]{4,3,2,1,0:T(8,128)(2,1)} %shard_map.55.green_ref, bf16[64,4,2,128,128]{4,3,2,1,0:T(8,128)(2,1)} %bitcast.25, bf16[128,128]{1,0:T(8,128)(2,1)} %copy.16.forward_ref, bf16[128,128]{1,0:T(8,128)(2,1)} %copy.17.mirrored_ref, ...), custom_call_target="tpu_custom_call" | custom-call | tf_op jit(solution)/shard_map/pallas_call | solution.py:335
  761.9 26.5 %shard_map.58 = bf16[4,4,2,512,512]{4,3,2,1,0:T(8,128)(2,1)} custom-call(bf16[16,8,4,4,2,16,128]{6,5,4,3,2,1,0:T(8,128)(2,1)} %shard_map.57.blocks_ref, bf16[512,512]{1,0:T(8,128)(2,1)} %coulomb_ref.1), custom_call_target="tpu_custom_call" | custom-call | tf_op jit(solution)/shard_map/pallas_call | solution.py:399
  (5 shorter events, 0.1 us)
